TPU v7x, 32 devices: a whole 2x2x4 slice. The times are simulated.
32 devices in a mesh: dp: 4 (over y, x), loop: 8 (over z, core).
Axes of the slice: x: 2, y: 2, z: 4, core: 2. Of those that a mesh axis runs over, the one named last changes fastest.
Arguments:
- features: bfloat16 [24, 7, 7, 2048], P('loop'), may hold values from -6 to 6
- image_ids: int32 [24], P('loop'), may hold values from 0 to 15
- text_embeds: bfloat16 [16, 1152], P('loop'), may hold values from -6 to 6
- text_ids: int32 [16], replicated, may hold values from 0 to 15, each once
- depth_kernel: bfloat16 [7, 7, 2048], replicated, may hold values from -0.875 to 0.875
- depth_bias: float32 [2048], replicated, may hold values from -3 to 3
- norm_gain: float32 [2048], replicated, may hold values from 0.5 to 2
- w_up: bfloat16 [2048, 4096], P(None, 'dp'), may hold values from -0.125 to 0.125
- w_down: bfloat16 [2048, 4096], P(None, 'dp'), may hold values from -0.09375 to 0.09375
- projection: bfloat16 [2048, 1152], replicated, may hold values from -0.125 to 0.125
- logit_scale: float32 [1], replicated, may hold values from 4 to 16
- logit_bias: float32 [1], replicated, may hold values from -4 to -1
Outputs:
- row_loss: float32 [24], P('loop')
- grad_texts: float32 [16, 1152], P('loop')
- grad_kernel: float32 [7, 7, 2048], replicated
- grad_bias: float32 [2048], replicated
- grad_gain: float32 [2048], replicated
- grad_up: float32 [2048, 4096], P('loop', 'dp')
- grad_down: float32 [2048, 4096], P('loop', 'dp')
- grad_proj: float32 [2048, 1152], P(('dp', 'loop'))
Inputs may be any that keep to these rules, and one draw needn't show every extreme that they name: `image_ids`: each image's pair id names one text. `text_ids`: the 16 texts carry distinct pair ids.
All inputs are finite; a program needn't handle non-finite values.
Results may differ from a plain program's by a relative error of at most 0.0065.
Values sent between devices are 32-bit elements; how exact they have to be, the bound alone decides.
A program may use at most 192 MiB of HBM per device.

v0:
```python
import jax
import jax.numpy as jnp
import numpy as np
from jax import lax
from jax.sharding import PartitionSpec as P

GRID = 7
full_precision = lax.Precision.HIGHEST
half_root = 0.7071067811865476
density_factor = 0.3989422804014327


def shifted(shard, axis, by):
    count = lax.axis_size(axis)
    return lax.ppermute(shard, axis, [(i, (i + by) % count) for i in range(count)])


def gelu_value(values):
    return 0.5 * values * (1.0 + lax.erf(values * half_root))


def gelu_slope(values):
    cumulative = 0.5 * (1.0 + lax.erf(values * half_root))
    return cumulative + values * jnp.exp(-0.5 * values * values) * density_factor


def depthwise(images, kernel):
    side = kernel.shape[0]
    reach = (side - 1) // 2
    height = images.shape[1]
    width = images.shape[2]
    padded = jnp.pad(images, ((0, 0), (reach, reach), (reach, reach), (0, 0)))
    total = jnp.zeros(images.shape, jnp.float32)
    for row_off in range(side):
        for col_off in range(side):
            window = padded[:, row_off : row_off + height, col_off : col_off + width, :].astype(
                jnp.float32
            )
            total = total + window * kernel[row_off, col_off]
    return total


def kernel_grad(images, grad_conv, side):
    reach = (side - 1) // 2
    height = images.shape[1]
    width = images.shape[2]
    padded = jnp.pad(images, ((0, 0), (reach, reach), (reach, reach), (0, 0)))
    positions = np.arange(width)
    rows_out = []
    for row_off in range(side):
        slab = padded[:, row_off : row_off + height, :, :].astype(jnp.float32)
        cross = jnp.einsum("npsc,npqc->sqc", slab, grad_conv, precision=full_precision)
        cols_out = []
        for col_off in range(side):
            cols_out.append(jnp.sum(cross[positions + col_off, positions], axis=0))
        rows_out.append(jnp.stack(cols_out, axis=0))
    return jnp.stack(rows_out, axis=0)


def norm_parts(images, depth_kernel, depth_bias, norm_gain):
    conv_out = depthwise(images, depth_kernel.astype(jnp.float32)) + depth_bias
    centered = conv_out - jnp.mean(conv_out, axis=3, keepdims=True)
    inv_std = lax.rsqrt(jnp.mean(centered * centered, axis=3, keepdims=True) + 1e-06)
    unit_part = centered * inv_std
    normed = (unit_part * norm_gain).astype(jnp.bfloat16)
    return (unit_part, inv_std, normed)


def unit_rows(values):
    inverse = lax.rsqrt(jnp.sum(values * values, axis=1, keepdims=True) + 1e-06)
    return (values * inverse, inverse)


def conv_grads(images, depth_kernel, unit_part, inv_std, norm_gain, grad_normed):
    grad_gain = jnp.sum(grad_normed * unit_part, axis=(0, 1, 2))
    grad_unit = grad_normed * norm_gain
    grad_conv = inv_std * (
        grad_unit
        - jnp.mean(grad_unit, axis=3, keepdims=True)
        - unit_part * jnp.mean(grad_unit * unit_part, axis=3, keepdims=True)
    )
    grad_bias = jnp.sum(grad_conv, axis=(0, 1, 2))
    grad_kernel = kernel_grad(images, grad_conv, depth_kernel.shape[0])
    return (grad_kernel, grad_bias, grad_gain)


def on_device(
    features,
    image_ids,
    text_embeds,
    text_ids,
    depth_kernel,
    depth_bias,
    norm_gain,
    w_up,
    w_down,
    projection,
    logit_scale,
    logit_bias,
):
    image_rows = features.shape[0]
    channels = features.shape[3]
    hidden_share = w_up.shape[1]
    cell_count = GRID * GRID
    loop_count = lax.axis_size("loop")
    position = lax.axis_index("loop")
    unit_part, inv_std, normed = norm_parts(features, depth_kernel, depth_bias, norm_gain)
    normed_rows = normed.reshape(-1, channels)
    pre_act = jnp.dot(normed_rows, w_up, preferred_element_type=jnp.float32)
    hidden_mean = jnp.mean(
        gelu_value(pre_act).reshape(image_rows, cell_count, hidden_share), axis=1
    ).astype(jnp.bfloat16)
    mlp_part = lax.dot_general(
        hidden_mean, w_down, (((1,), (1,)), ((), ())), preferred_element_type=jnp.float32
    )
    mlp_pool = lax.psum(mlp_part, "dp")
    pooled = (jnp.mean(features.astype(jnp.float32), axis=(1, 2)) + mlp_pool).astype(jnp.bfloat16)
    embedding = jnp.dot(pooled, projection, preferred_element_type=jnp.float32)
    image_unit, image_inverse = unit_rows(embedding)
    text_unit, text_inverse = unit_rows(text_embeds.astype(jnp.float32))
    text_rows = text_embeds.shape[0]
    embed_width = text_embeds.shape[1]
    scale_value = logit_scale[0]
    bias_value = logit_bias[0]

    def pair_tile(block_unit, first_text):
        block_ids = lax.dynamic_slice_in_dim(text_ids, first_text, block_unit.shape[0])
        logits = (
            scale_value * jnp.dot(image_unit, block_unit.T, precision=full_precision) + bias_value
        )
        labels = jnp.where(image_ids[:, None] == block_ids[None, :], 1.0, -1.0).astype(jnp.float32)
        loss_part = -jnp.sum(jax.nn.log_sigmoid(labels * logits), axis=1)
        coeffs = -scale_value * labels * jax.nn.sigmoid(-labels * logits)
        return (loss_part, coeffs)

    def loop_turn(turn_index, carry_state):
        moving, loss_sum, grad_image = carry_state
        block_unit = moving[:text_rows]
        block_grad = moving[text_rows:]
        source = (position - turn_index) % loop_count
        loss_part, coeffs = pair_tile(block_unit, source * text_rows)
        grad_image = grad_image + jnp.dot(coeffs, block_unit, precision=full_precision)
        block_grad = block_grad + jnp.dot(coeffs.T, image_unit, precision=full_precision)
        stacked = jnp.concatenate([block_unit, block_grad], axis=0)
        moving = shifted(stacked, "loop", 1)
        return (moving, loss_sum + loss_part, grad_image)

    start_state = (
        jnp.concatenate([text_unit, jnp.zeros((text_rows, embed_width), jnp.float32)], axis=0),
        jnp.zeros((image_rows,), jnp.float32),
        jnp.zeros((image_rows, embed_width), jnp.float32),
    )
    moving, row_loss, grad_image = lax.fori_loop(0, loop_count, loop_turn, start_state)
    grad_text = moving[text_rows:]
    grad_texts = text_inverse * (
        grad_text - text_unit * jnp.sum(text_unit * grad_text, axis=1, keepdims=True)
    )
    grad_embed = (
        image_inverse
        * (grad_image - image_unit * jnp.sum(image_unit * grad_image, axis=1, keepdims=True))
    ).astype(jnp.bfloat16)
    grad_pooled = lax.dot_general(
        grad_embed, projection, (((1,), (1,)), ((), ())), preferred_element_type=jnp.float32
    ).astype(jnp.bfloat16)
    spread = jnp.dot(grad_pooled, w_down, preferred_element_type=jnp.float32) / cell_count
    grad_pre = (
        (gelu_slope(pre_act).reshape(image_rows, cell_count, hidden_share) * spread[:, None, :])
        .reshape(-1, hidden_share)
        .astype(jnp.bfloat16)
    )
    grad_normed = lax.dot_general(
        grad_pre, w_up, (((1,), (1,)), ((), ())), preferred_element_type=jnp.float32
    ).reshape(features.shape)
    kernel_part, bias_part, gain_part = conv_grads(
        features, depth_kernel, unit_part, inv_std, norm_gain, grad_normed
    )
    grad_kernel, grad_bias, grad_gain = lax.psum(
        (kernel_part, bias_part, gain_part), ("dp", "loop")
    )
    down_term = lax.dot_general(
        grad_pooled, hidden_mean, (((0,), (0,)), ((), ())), preferred_element_type=jnp.float32
    )
    row_share = channels // lax.axis_size("dp")
    pooled_share = lax.dynamic_slice_in_dim(pooled, lax.axis_index("dp") * row_share, row_share, 1)
    proj_term = lax.dot_general(
        pooled_share, grad_embed, (((0,), (0,)), ((), ())), preferred_element_type=jnp.float32
    )
    up_term = lax.dot_general(
        normed_rows, grad_pre, (((0,), (0,)), ((), ())), preferred_element_type=jnp.float32
    )
    grad_up, grad_down, grad_proj = (
        lax.psum_scatter(up_term, "loop", scatter_dimension=0, tiled=True),
        lax.psum_scatter(down_term, "loop", scatter_dimension=0, tiled=True),
        lax.psum_scatter(proj_term, "loop", scatter_dimension=0, tiled=True),
    )
    return (row_loss, grad_texts, grad_kernel, grad_bias, grad_gain, grad_up, grad_down, grad_proj)


def solution(mesh):
    placed = (
        P("loop", None, None, None),
        P("loop"),
        P("loop", None),
        P(),
        P(),
        P(),
        P(),
        P(None, "dp"),
        P(None, "dp"),
        P(),
        P(),
        P(),
    )
    return jax.shard_map(
        on_device,
        mesh=mesh,
        in_specs=placed,
        out_specs=(
            P("loop"),
            P("loop", None),
            P(),
            P(),
            P(),
            P("loop", "dp"),
            P("loop", "dp"),
            P(("dp", "loop"), None),
        ),
        check_vma=False,
    )
```

profile of v0, /device:TPU:1, one launch (start us, length us, event | category | flops | bytes accessed | tf_op | source)
XLA Modules:
  0.0 731.8 jit_solution(5146053782400025438)
XLA Ops:
  20.8 12.0 %fusion.60 = (f32[3,7,7]{2,1,0:T(8,128)S(1)}, f32[3,7,7,2048]{3,2,1,0:T(8,128)S(1)}) fusion(f32[2048]{0:T(1024)} %param.167, f32[2048]{0:T(1024)} %bitcast.201, f32[2048]{0:T(1024)} %bitcast.200, f32[2048]{0:T(1024)} %bitcast.199, f32[2048]{0:T(1024)} %bitcast.198, f32[2048]{0:T(1024)} %bitcast.197, f32[2048]{0:T(1024)} %bitcast.196, ...), kind=kLoop, calls=%fused_computation.218 | loop fusion | flops 44556140 | bytes 2216524 | tf_op jit(solution)/shard_map/reduce_sum | solution.py:62
  44.6 13.7 %psum.28 = f32[3,2048]{1,0:T(4,128)S(1)} all-reduce(f32[3,2048]{1,0:T(4,128)S(1)} %fusion.51), channel_id=1, replica_groups=mesh['dp'=4,'loop'=8] {'dp'}, use_global_device_ids=true, to_apply=%region_5.6 | all-reduce | flops 6144 | bytes 49152 | tf_op jit(solution)/shard_map/psum | solution.py:116
  61.6 55.7 %while.20 = (s32[]{:T(128)}, f32[4,1152]{1,0:T(4,128)S(1)}, f32[3]{0:T(128)S(1)}, f32[3,1152]{1,0:T(4,128)S(1)}, f32[]{:T(128)}, /*index=5*/s32[3]{0:T(128)S(1)}...) while((s32[]{:T(128)}, f32[4,1152]{1,0:T(4,128)S(1)}, ...), condition=%wide.region_9.10_spmd.clone, body=%wide.region_7.9_spmd.clone.sunk | while | flops 262864 | bytes 270863 | solution.py:153
  63.6 5.7 collective-permute-start
  91.9 4.6 collective-permute-done
  98.8 4.6 collective-permute-done
  112.7 4.6 collective-permute-done
  125.3 4.9 multiply_reduce_fusion
  132.5 14.9 %copy.168 = f32[3,7,7,2048]{1,2,0,3:T(8,128)} copy(f32[3,7,7,2048]{3,2,1,0:T(8,128)} %get-tuple-element.326) | data formatting | bytes 2408448 | tf_op jit(solution)/shard_map/mul | solution.py:77
  147.4 11.5 %copy.169 = bf16[3,7,13,2048]{2,1,0,3:T(8,128)(2,1)} copy(bf16[3,7,13,2048]{3,2,1,0:T(8,128)(2,1)S(1)} %copy-done.6) | data formatting | bytes 2236416 | tf_op jit(solution)/shard_map/slice | solution.py:51
  158.9 23.4 %convolution_bitcast_fusion.6 = f32[13,7,2048]{0,1,2:T(8,128)} fusion(f32[3,7,7,2048]{1,2,0,3:T(8,128)} %copy.168, bf16[3,7,13,2048]{2,1,0,3:T(8,128)(2,1)} %copy.169), kind=kOutput, calls=%fused_computation.133 | convolution fusion | flops 46964736 | bytes 3067904 | tf_op jit(solution)/shard_map/npsc,npqc->sqc/dot_general | solution.py:52
  182.3 5.3 copy.170
  190.2 13.0 %copy.178 = bf16[3,7,13,2048]{2,1,0,3:T(8,128)(2,1)} copy(bf16[3,7,13,2048]{3,2,1,0:T(8,128)(2,1)} %get-tuple-element.333) | data formatting | bytes 2236416 | tf_op jit(solution)/shard_map/slice | solution.py:51
  203.1 23.5 %convolution_bitcast_fusion.5 = f32[13,7,2048]{0,1,2:T(8,128)} fusion(f32[3,7,7,2048]{1,2,0,3:T(8,128)} %copy.168, bf16[3,7,13,2048]{2,1,0,3:T(8,128)(2,1)} %copy.178), kind=kOutput, calls=%fused_computation.132 | convolution fusion | flops 46964736 | bytes 3067904 | tf_op jit(solution)/shard_map/npsc,npqc->sqc/dot_general | solution.py:52
  226.6 5.3 copy.179
  246.2 13.0 %copy.187 = bf16[3,7,13,2048]{2,1,0,3:T(8,128)(2,1)} copy(bf16[3,7,13,2048]{3,2,1,0:T(8,128)(2,1)} %get-tuple-element.334) | data formatting | bytes 2236416 | tf_op jit(solution)/shard_map/slice | solution.py:51
  259.1 23.7 %convolution_bitcast_fusion.4 = f32[13,7,2048]{0,1,2:T(8,128)} fusion(f32[3,7,7,2048]{1,2,0,3:T(8,128)} %copy.168, bf16[3,7,13,2048]{2,1,0,3:T(8,128)(2,1)} %copy.187), kind=kOutput, calls=%fused_computation.131 | convolution fusion | flops 46964736 | bytes 3067904 | tf_op jit(solution)/shard_map/npsc,npqc->sqc/dot_general | solution.py:52
  282.8 5.3 copy.188
  296.8 13.0 %copy.196 = bf16[3,7,13,2048]{2,1,0,3:T(8,128)(2,1)} copy(bf16[3,7,13,2048]{3,2,1,0:T(8,128)(2,1)} %get-tuple-element.335) | data formatting | bytes 2236416 | tf_op jit(solution)/shard_map/slice | solution.py:51
  309.7 23.3 %convolution_bitcast_fusion.3 = f32[13,7,2048]{0,1,2:T(8,128)} fusion(f32[3,7,7,2048]{1,2,0,3:T(8,128)} %copy.168, bf16[3,7,13,2048]{2,1,0,3:T(8,128)(2,1)} %copy.196), kind=kOutput, calls=%fused_computation.130 | convolution fusion | flops 46964736 | bytes 3067904 | tf_op jit(solution)/shard_map/npsc,npqc->sqc/dot_general | solution.py:52
  333.1 5.3 copy.197
  347.0 11.5 %copy.205 = bf16[3,7,13,2048]{2,1,0,3:T(8,128)(2,1)} copy(bf16[3,7,13,2048]{3,2,1,0:T(8,128)(2,1)S(1)} %get-tuple-element.336) | data formatting | bytes 2236416 | tf_op jit(solution)/shard_map/slice | solution.py:51
  358.5 23.4 %convolution_bitcast_fusion.2 = f32[13,7,2048]{0,1,2:T(8,128)} fusion(f32[3,7,7,2048]{1,2,0,3:T(8,128)} %copy.168, bf16[3,7,13,2048]{2,1,0,3:T(8,128)(2,1)} %copy.205), kind=kOutput, calls=%fused_computation.129 | convolution fusion | flops 46964736 | bytes 3067904 | tf_op jit(solution)/shard_map/npsc,npqc->sqc/dot_general | solution.py:52
  381.9 5.3 copy.206
  392.3 11.5 %copy.214 = bf16[3,7,13,2048]{2,1,0,3:T(8,128)(2,1)} copy(bf16[3,7,13,2048]{3,2,1,0:T(8,128)(2,1)S(1)} %copy-done.5) | data formatting | bytes 2236416 | tf_op jit(solution)/shard_map/slice | solution.py:51
  403.8 23.4 %convolution_bitcast_fusion.1 = f32[13,7,2048]{0,1,2:T(8,128)} fusion(f32[3,7,7,2048]{1,2,0,3:T(8,128)} %copy.168, bf16[3,7,13,2048]{2,1,0,3:T(8,128)(2,1)} %copy.214), kind=kOutput, calls=%fused_computation.128 | convolution fusion | flops 46964736 | bytes 3067904 | tf_op jit(solution)/shard_map/npsc,npqc->sqc/dot_general | solution.py:52
  427.2 5.3 copy.215
  437.6 11.5 %copy.223 = bf16[3,7,13,2048]{2,1,0,3:T(8,128)(2,1)} copy(bf16[3,7,13,2048]{3,2,1,0:T(8,128)(2,1)S(1)} %copy-done.4) | data formatting | bytes 2236416 | tf_op jit(solution)/shard_map/slice | solution.py:51
  449.1 23.5 %convolution_bitcast_fusion = f32[13,7,2048]{0,1,2:T(8,128)} fusion(f32[3,7,7,2048]{1,2,0,3:T(8,128)} %copy.168, bf16[3,7,13,2048]{2,1,0,3:T(8,128)(2,1)} %copy.223), kind=kOutput, calls=%fused_computation.127 | convolution fusion | flops 46964736 | bytes 3067904 | tf_op jit(solution)/shard_map/npsc,npqc->sqc/dot_general | solution.py:52
  472.5 5.3 copy.224
  505.4 41.1 %all-reduce.2 = (f32[2048]{0:T(1024)}, f32[2048]{0:T(1024)}) all-reduce(f32[2048]{0:T(1024)S(1)} %copy-done.67, f32[2048]{0:T(1024)S(1)} %copy-done.66), channel_id=1, replica_groups=mesh['dp'=4,'loop'=8] {'dp','loop'}, use_global_device_ids=true, to_apply=%region_65.66 | all-reduce | flops 4096 | bytes 32768 | tf_op jit(solution)/shard_map/psum | solution.py:177
  547.4 174.4 %all-reduce.5.cloned.1.call-done = f32[7,7,2048]{2,1,0:T(8,128)} async-done(((f32[7,7,2048]{2,1,0:T(8,128)}), f32[7,7,2048]{2,1,0:T(8,128)}) %all-reduce.5.cloned.1.call-update) | async-done | bytes 401424 | tf_op jit(solution)/shard_map/psum | solution.py:177
  (393 shorter events, 146.4 us)
Async XLA Ops:
  8.0 7.8 %copy-start.3 = (bf16[3,7,7,2048]{3,2,1,0:T(8,128)(2,1)S(1)}, bf16[3,7,7,2048]{3,2,1,0:T(8,128)(2,1)}, u32[]{:S(2)}) copy-start(bf16[3,7,7,2048]{3,2,1,0:T(8,128)(2,1)} %param.162) | copy-start | bytes 1806340
  8.0 713.9 %all-reduce.5.cloned.1.call-start = ((), (), s32[]{:S(2)}) async-start(), calls=%async_computation.3 | async-start | bytes 917504 | tf_op jit(solution)/shard_map/psum | solution.py:177
  20.1 13.1 %copy-start.71 = (f32[2]{0:T(128)}, f32[2]{0:T(128)S(1)}, u32[]{:S(2)}) copy-start(f32[2]{0:T(128)S(1)} %add_rsqrt_fusion.2) | copy-start | bytes 28
  20.8 12.4 %copy-start.57 = (f32[2048]{0:T(1024)S(1)}, f32[2048]{0:T(1024)}, u32[]{:S(2)}) copy-start(f32[2048]{0:T(1024)} %param.168) | copy-start | bytes 24580
  41.2 17.1 %copy-start.62 = (f32[3,2048]{1,0:T(4,128)S(1)}, f32[3,2048]{1,0:T(4,128)}, u32[]{:S(2)}) copy-start(f32[3,2048]{1,0:T(4,128)} %convert_reduce_fusion) | copy-start | bytes 73732
  61.5 59.8 %copy-start.16 = (f32[3,1152]{1,0:T(4,128)}, f32[3,1152]{1,0:T(4,128)S(1)}, u32[]{:S(2)}) copy-start(f32[3,1152]{1,0:T(4,128)S(1)} %get-tuple-element.390) | copy-start | bytes 41476
  61.6 59.8 %copy-start.68 = (f32[3]{0:T(128)}, f32[3]{0:T(128)S(1)}, u32[]{:S(2)}) copy-start(f32[3]{0:T(128)S(1)} %add_rsqrt_fusion.1) | copy-start | bytes 40
  63.6 6.6 collective-permute-start
  72.0 3.7 collective-permute-start
  77.6 5.0 collective-permute-start
  84.5 5.0 collective-permute-start
  91.5 5.0 collective-permute-start
  98.4 5.0 collective-permute-start
  105.4 5.0 collective-permute-start
  112.3 5.0 collective-permute-start
  132.5 14.9 %copy-start.6 = (bf16[3,7,13,2048]{3,2,1,0:T(8,128)(2,1)S(1)}, bf16[3,7,13,2048]{3,2,1,0:T(8,128)(2,1)}, u32[]{:S(2)}) copy-start(bf16[3,7,13,2048]{3,2,1,0:T(8,128)(2,1)} %get-tuple-element.332) | copy-start | bytes 3354628
  182.3 6.6 copy-start.14
  226.6 7.2 copy-start.13
  233.2 5.6 copy-start.11
  235.0 6.2 copy-start.10
  237.5 6.2 copy-start.9
  480.3 6.3 copy-start.49
  480.3 6.3 copy-start.48
  481.6 5.2 copy-start.52
  481.6 5.3 copy-start.53
  481.6 5.3 copy-start.54
  491.0 230.8 %reduce-scatter.8.cloned.1.call-start = ((), (), s32[]{:S(2)}) async-start(), calls=%async_computation.6 | async-start | bytes 2654208 | tf_op jit(solution)/shard_map/reduce_scatter | solution.py:194
  493.8 228.1 %reduce-scatter.4.cloned.1.call-start = ((), (), s32[]{:S(2)}) async-start(), calls=%async_computation.4 | async-start | bytes 9437184 | tf_op jit(solution)/shard_map/reduce_scatter | solution.py:192
  499.5 222.4 %reduce-scatter.6.cloned.1.call-start = ((), (), s32[]{:S(2)}) async-start(), calls=%async_computation.5 | async-start | bytes 9437184 | tf_op jit(solution)/shard_map/reduce_scatter | solution.py:193
  504.7 41.8 %copy-start.19 = (f32[4,1152]{1,0:T(4,128)S(1)}, f32[4,1152]{1,0:T(4,128)}, u32[]{:S(2)}) copy-start(f32[4,1152]{1,0:T(4,128)} %copy-done.18) | copy-start | bytes 55300
  504.7 41.9 %copy-start.65 = (bf16[2,1152]{1,0:T(2,128)(2,1)S(1)}, bf16[2,1152]{1,0:T(2,128)(2,1)}, u32[]{:S(2)}) copy-start(bf16[2,1152]{1,0:T(2,128)(2,1)} %param.164) | copy-start | bytes 13828
  504.7 41.8 %copy-start.72 = (f32[2]{0:T(128)S(1)}, f32[2]{0:T(128)}, u32[]{:S(2)}) copy-start(f32[2]{0:T(128)} %copy-done.71) | copy-start | bytes 28
  (57 other events, 172.5 us)
Sparse Core Ops, SparseCore 0:
  491.2 230.6 all-reduce.4
Sparse Core Ops, SparseCore 1:
  494.5 34.6 reduce-scatter.7
  532.0 89.7 reduce-scatter.3
  624.7 90.0 reduce-scatter.5
where the time goes:
time: 739 us; the launch traced here: 732 us
  matrix products  213 us (29%)
  local copies, waits for them, and re-layouts  210 us (28%)
  waiting for transfers between devices  202 us (27%)
  blocking collectives  54.8 us (7%)
  other arithmetic  22.8 us (3%)
  between operations  18.2 us (2%)
  starting transfers between devices  10.5 us (1%)
    psum x1, waiting for transfers between devices, on_device(): lax.psum((kernel_part, bias_part, gain_part), ('dp', 'loop'))  174 us
    dot_general x7, matrix products, kernel_grad(): jnp.einsum('npsc,npqc->sqc', slab, grad_conv, precision=full_precision)  164 us
    slice x8, local copies, waits for them, and re-layouts, kernel_grad(): slab = padded[:, row_off:row_off + height, :, :].astype(jnp.float32)  89 us
    gather x49, local copies, waits for them, and re-layouts, kernel_grad(): cols_out.append(jnp.sum(cross[positions + col_off, positions], axis=0))  52.7 us
    psum x1, blocking collectives, on_device(): lax.psum((kernel_part, bias_part, gain_part), ('dp', 'loop'))  41.1 us
    transpose x7, local copies, waits for them, and re-layouts, kernel_grad(): jnp.einsum('npsc,npqc->sqc', slab, grad_conv, precision=full_precision)  37.1 us
    ppermute x8, waiting for transfers between devices, shifted(): lax.ppermute(shard, axis, [(i, (i + by) % count) for i in range(count)])  27.2 us
    mul x1, local copies, waits for them, and re-layouts, conv_grads(): inv_std * (grad_unit - jnp.mean(grad_unit, axis=3, keepdims=True) - unit_...  14.9 us
  transfers between devices with their start and end apart: 12, of which 9 were waited for; matrix products, arithmetic and copies ran while one was open for 2% of the time, Pallas kernels for 0%

commit v1 on v0

--- a/solution.py
+++ b/solution.py
@@ -8,6 +8,11 @@
 full_precision = lax.Precision.HIGHEST
 half_root = 0.7071067811865476
 density_factor = 0.3989422804014327
+
+
+def one_after_other(array, first, second):
+    inner = lax.psum(array, first)
+    return lax.psum(inner, second)
 
 
 def shifted(shard, axis, by):
@@ -174,8 +179,8 @@
     kernel_part, bias_part, gain_part = conv_grads(
         features, depth_kernel, unit_part, inv_std, norm_gain, grad_normed
     )
-    grad_kernel, grad_bias, grad_gain = lax.psum(
-        (kernel_part, bias_part, gain_part), ("dp", "loop")
+    grad_kernel, grad_bias, grad_gain = one_after_other(
+        (kernel_part, bias_part, gain_part), "loop", "dp"
     )
     down_term = lax.dot_general(
         grad_pooled, hidden_mean, (((0,), (0,)), ((), ())), preferred_element_type=jnp.float32

time: 739 us -> 832 us (1.13)
  waiting for transfers between devices: 202 us -> 297 us
    psum x1 -> x2, waiting for transfers between devices: 174 us -> 54.2 us  [the longest x1 54.2 us: one_after_other(): inner = lax.psum(array, first)]
    reduce_scatter x1, waiting for transfers between devices: 0.01 us -> 91.8 us  [on_device(): lax.psum_scatter(up_term, 'loop', scatter_dimension=0, tiled=True)]
    reduce_scatter x1, waiting for transfers between devices: 0.01 us -> 90.7 us  [on_device(): lax.psum_scatter(down_term, 'loop', scatter_dimension=0, tiled=True)]
    reduce_scatter x1, waiting for transfers between devices: 0.01 us -> 33.2 us  [on_device(): lax.psum_scatter(proj_term, 'loop', scatter_dimension=0, tiled=True)]
    psum x1 -> x2, blocking collectives: 41.1 us -> 37.1 us  [the longest x1 24.2 us: one_after_other(): inner = lax.psum(array, first)]
  transfers between devices with their start and end apart: 12 -> 13, of which waited for: 9 -> 12; matrix products, arithmetic and copies ran while one was open for 2% -> 2% of each run, Pallas kernels for 0% -> 0%
where the time goes in v1:
time: 832 us; the launch traced here: 822 us
  waiting for transfers between devices  297 us (36%)
  matrix products  213 us (26%)
  local copies, waits for them, and re-layouts  206 us (25%)
  blocking collectives  50.7 us (6%)
  other arithmetic  27.9 us (3%)
  between operations  16.2 us (2%)
  starting transfers between devices  10.5 us (1%)
    dot_general x7, matrix products, kernel_grad(): jnp.einsum('npsc,npqc->sqc', slab, grad_conv, precision=full_precision)  164 us
    reduce_scatter x1, waiting for transfers between devices, on_device(): lax.psum_scatter(up_term, 'loop', scatter_dimension=0, tiled=True)  91.8 us
    reduce_scatter x1, waiting for transfers between devices, on_device(): lax.psum_scatter(down_term, 'loop', scatter_dimension=0, tiled=True)  90.7 us
    slice x8, local copies, waits for them, and re-layouts, kernel_grad(): slab = padded[:, row_off:row_off + height, :, :].astype(jnp.float32)  89 us
    psum x1, waiting for transfers between devices, one_after_other(): inner = lax.psum(array, first)  54.2 us
    gather x49, local copies, waits for them, and re-layouts, kernel_grad(): cols_out.append(jnp.sum(cross[positions + col_off, positions], axis=0))  48.4 us
    transpose x7, local copies, waits for them, and re-layouts, kernel_grad(): jnp.einsum('npsc,npqc->sqc', slab, grad_conv, precision=full_precision)  37.1 us
    reduce_scatter x1, waiting for transfers between devices, on_device(): lax.psum_scatter(proj_term, 'loop', scatter_dimension=0, tiled=True)  33.2 us
  transfers between devices with their start and end apart: 13, of which 12 were waited for; matrix products, arithmetic and copies ran while one was open for 2% of the time, Pallas kernels for 0%

profile of v1, /device:TPU:1, one launch (start us, length us, event | category | flops | bytes accessed | tf_op | source)
XLA Modules:
  0.0 822.0 jit_solution(12358572630466767126)
XLA Ops:
  20.0 12.0 %fusion.60 = (f32[3,7,7]{2,1,0:T(8,128)S(1)}, f32[3,7,7,2048]{3,2,1,0:T(8,128)S(1)}) fusion(f32[2048]{0:T(1024)} %param.167, f32[2048]{0:T(1024)} %bitcast.201, f32[2048]{0:T(1024)} %bitcast.200, f32[2048]{0:T(1024)} %bitcast.199, f32[2048]{0:T(1024)} %bitcast.198, f32[2048]{0:T(1024)} %bitcast.197, f32[2048]{0:T(1024)} %bitcast.196, ...), kind=kLoop, calls=%fused_computation.218 | loop fusion | flops 44556140 | bytes 2216524 | tf_op jit(solution)/shard_map/reduce_sum | solution.py:67
  43.8 13.7 %psum.49 = f32[3,2048]{1,0:T(4,128)S(1)} all-reduce(f32[3,2048]{1,0:T(4,128)S(1)} %fusion.51), channel_id=1, replica_groups=mesh['dp'=4,'loop'=8] {'dp'}, use_global_device_ids=true, to_apply=%region_5.6 | all-reduce | flops 6144 | bytes 49152 | tf_op jit(solution)/shard_map/psum | solution.py:121
  60.8 55.7 %while.20 = (s32[]{:T(128)}, f32[4,1152]{1,0:T(4,128)S(1)}, f32[3]{0:T(128)S(1)}, f32[3,1152]{1,0:T(4,128)S(1)}, f32[]{:T(128)}, /*index=5*/s32[3]{0:T(128)S(1)}...) while((s32[]{:T(128)}, f32[4,1152]{1,0:T(4,128)S(1)}, ...), condition=%wide.region_9.10_spmd.clone, body=%wide.region_7.9_spmd.clone.sunk | while | flops 262864 | bytes 270863 | solution.py:158
  62.7 5.7 collective-permute-start
  131.7 14.9 %copy.168 = f32[3,7,7,2048]{1,2,0,3:T(8,128)} copy(f32[3,7,7,2048]{3,2,1,0:T(8,128)} %get-tuple-element.328) | data formatting | bytes 2408448 | tf_op jit(solution)/shard_map/mul | solution.py:82
  146.6 11.5 %copy.169 = bf16[3,7,13,2048]{2,1,0,3:T(8,128)(2,1)} copy(bf16[3,7,13,2048]{3,2,1,0:T(8,128)(2,1)S(1)} %copy-done.6) | data formatting | bytes 2236416 | tf_op jit(solution)/shard_map/slice | solution.py:56
  158.1 23.4 %convolution_bitcast_fusion.6 = f32[13,7,2048]{0,1,2:T(8,128)} fusion(f32[3,7,7,2048]{1,2,0,3:T(8,128)} %copy.168, bf16[3,7,13,2048]{2,1,0,3:T(8,128)(2,1)} %copy.169), kind=kOutput, calls=%fused_computation.133 | convolution fusion | flops 46964736 | bytes 3067904 | tf_op jit(solution)/shard_map/npsc,npqc->sqc/dot_general | solution.py:57
  181.5 5.3 copy.170
  189.3 13.0 %copy.178 = bf16[3,7,13,2048]{2,1,0,3:T(8,128)(2,1)} copy(bf16[3,7,13,2048]{3,2,1,0:T(8,128)(2,1)} %get-tuple-element.335) | data formatting | bytes 2236416 | tf_op jit(solution)/shard_map/slice | solution.py:56
  202.3 23.5 %convolution_bitcast_fusion.5 = f32[13,7,2048]{0,1,2:T(8,128)} fusion(f32[3,7,7,2048]{1,2,0,3:T(8,128)} %copy.168, bf16[3,7,13,2048]{2,1,0,3:T(8,128)(2,1)} %copy.178), kind=kOutput, calls=%fused_computation.132 | convolution fusion | flops 46964736 | bytes 3067904 | tf_op jit(solution)/shard_map/npsc,npqc->sqc/dot_general | solution.py:57
  225.7 5.3 copy.179
  245.3 13.0 %copy.187 = bf16[3,7,13,2048]{2,1,0,3:T(8,128)(2,1)} copy(bf16[3,7,13,2048]{3,2,1,0:T(8,128)(2,1)} %get-tuple-element.336) | data formatting | bytes 2236416 | tf_op jit(solution)/shard_map/slice | solution.py:56
  258.3 23.7 %convolution_bitcast_fusion.4 = f32[13,7,2048]{0,1,2:T(8,128)} fusion(f32[3,7,7,2048]{1,2,0,3:T(8,128)} %copy.168, bf16[3,7,13,2048]{2,1,0,3:T(8,128)(2,1)} %copy.187), kind=kOutput, calls=%fused_computation.131 | convolution fusion | flops 46964736 | bytes 3067904 | tf_op jit(solution)/shard_map/npsc,npqc->sqc/dot_general | solution.py:57
  282.0 5.3 copy.188
  295.9 13.0 %copy.196 = bf16[3,7,13,2048]{2,1,0,3:T(8,128)(2,1)} copy(bf16[3,7,13,2048]{3,2,1,0:T(8,128)(2,1)} %get-tuple-element.337) | data formatting | bytes 2236416 | tf_op jit(solution)/shard_map/slice | solution.py:56
  308.9 23.3 %convolution_bitcast_fusion.3 = f32[13,7,2048]{0,1,2:T(8,128)} fusion(f32[3,7,7,2048]{1,2,0,3:T(8,128)} %copy.168, bf16[3,7,13,2048]{2,1,0,3:T(8,128)(2,1)} %copy.196), kind=kOutput, calls=%fused_computation.130 | convolution fusion | flops 46964736 | bytes 3067904 | tf_op jit(solution)/shard_map/npsc,npqc->sqc/dot_general | solution.py:57
  332.2 5.3 copy.197
  346.2 11.5 %copy.205 = bf16[3,7,13,2048]{2,1,0,3:T(8,128)(2,1)} copy(bf16[3,7,13,2048]{3,2,1,0:T(8,128)(2,1)S(1)} %get-tuple-element.338) | data formatting | bytes 2236416 | tf_op jit(solution)/shard_map/slice | solution.py:56
  357.7 23.4 %convolution_bitcast_fusion.2 = f32[13,7,2048]{0,1,2:T(8,128)} fusion(f32[3,7,7,2048]{1,2,0,3:T(8,128)} %copy.168, bf16[3,7,13,2048]{2,1,0,3:T(8,128)(2,1)} %copy.205), kind=kOutput, calls=%fused_computation.129 | convolution fusion | flops 46964736 | bytes 3067904 | tf_op jit(solution)/shard_map/npsc,npqc->sqc/dot_general | solution.py:57
  381.1 5.3 copy.206
  390.8 11.5 %copy.214 = bf16[3,7,13,2048]{2,1,0,3:T(8,128)(2,1)} copy(bf16[3,7,13,2048]{3,2,1,0:T(8,128)(2,1)S(1)} %copy-done.5) | data formatting | bytes 2236416 | tf_op jit(solution)/shard_map/slice | solution.py:56
  402.4 23.4 %convolution_bitcast_fusion.1 = f32[13,7,2048]{0,1,2:T(8,128)} fusion(f32[3,7,7,2048]{1,2,0,3:T(8,128)} %copy.168, bf16[3,7,13,2048]{2,1,0,3:T(8,128)(2,1)} %copy.214), kind=kOutput, calls=%fused_computation.128 | convolution fusion | flops 46964736 | bytes 3067904 | tf_op jit(solution)/shard_map/npsc,npqc->sqc/dot_general | solution.py:57
  425.8 5.3 copy.215
  435.5 11.5 %copy.223 = bf16[3,7,13,2048]{2,1,0,3:T(8,128)(2,1)} copy(bf16[3,7,13,2048]{3,2,1,0:T(8,128)(2,1)S(1)} %copy-done.4) | data formatting | bytes 2236416 | tf_op jit(solution)/shard_map/slice | solution.py:56
  447.1 23.5 %convolution_bitcast_fusion = f32[13,7,2048]{0,1,2:T(8,128)} fusion(f32[3,7,7,2048]{1,2,0,3:T(8,128)} %copy.168, bf16[3,7,13,2048]{2,1,0,3:T(8,128)(2,1)} %copy.223), kind=kOutput, calls=%fused_computation.127 | convolution fusion | flops 46964736 | bytes 3067904 | tf_op jit(solution)/shard_map/npsc,npqc->sqc/dot_general | solution.py:57
  470.5 5.3 copy.224
  490.9 54.2 %all-reduce.7.cloned.1.call-done = f32[7,7,2048]{2,1,0:T(8,128)} async-done(((f32[7,7,2048]{2,1,0:T(8,128)}), f32[7,7,2048]{2,1,0:T(8,128)}) %all-reduce.7.cloned.1.call-update) | async-done | bytes 401424 | tf_op jit(solution)/shard_map/psum | solution.py:14
  559.5 24.2 %all-reduce.2 = (f32[2048]{0:T(1024)S(1)}, f32[2048]{0:T(1024)S(1)}) all-reduce(f32[2048]{0:T(1024)S(1)} %copy-done.54, f32[2048]{0:T(1024)S(1)} %copy-done.53), channel_id=1, replica_groups=mesh['dp'=4,'loop'=8] {'loop'}, use_global_device_ids=true, to_apply=%region_66.67 | all-reduce | flops 4096 | bytes 32768 | tf_op jit(solution)/shard_map/psum | solution.py:14
  583.7 12.9 %all-reduce.3 = (f32[2048]{0:T(1024)}, f32[2048]{0:T(1024)}) all-reduce(f32[2048]{0:T(1024)S(1)} %get-tuple-element.323, f32[2048]{0:T(1024)S(1)} %get-tuple-element.324), channel_id=1, replica_groups=mesh['dp'=4,'loop'=8] {'dp'}, use_global_device_ids=true, to_apply=%region_67.68 | all-reduce | flops 4096 | bytes 32768 | tf_op jit(solution)/shard_map/psum | solution.py:15
  597.4 33.2 %reduce-scatter.8.cloned.1.call-done = f32[64,1152]{1,0:T(8,128)} async-done(((f32[512,1152]{1,0:T(8,128)}), f32[64,1152]{1,0:T(8,128)}) %reduce-scatter.8.cloned.1.call-update) | async-done | bytes 294928 | tf_op jit(solution)/shard_map/reduce_scatter | solution.py:199
  630.6 91.8 %reduce-scatter.4.cloned.1.call-done = f32[256,1024]{1,0:T(8,128)} async-done(((f32[2048,1024]{1,0:T(8,128)}), f32[256,1024]{1,0:T(8,128)}) %reduce-scatter.4.cloned.1.call-update) | async-done | bytes 1048592 | tf_op jit(solution)/shard_map/reduce_scatter | solution.py:197
  722.4 90.7 %reduce-scatter.6.cloned.1.call-done = f32[256,1024]{1,0:T(8,128)} async-done(((f32[2048,1024]{1,0:T(8,128)}), f32[256,1024]{1,0:T(8,128)}) %reduce-scatter.6.cloned.1.call-update) | async-done | bytes 1048592 | tf_op jit(solution)/shard_map/reduce_scatter | solution.py:198
  (371 shorter events, 165.9 us)
Async XLA Ops:
  7.2 537.9 %all-reduce.7.cloned.1.call-start = ((), (), s32[]{:S(2)}) async-start(), calls=%async_computation.3 | async-start | bytes 917504 | tf_op jit(solution)/shard_map/psum | solution.py:14
  19.3 13.1 %copy-start.58 = (f32[2]{0:T(128)}, f32[2]{0:T(128)S(1)}, u32[]{:S(2)}) copy-start(f32[2]{0:T(128)S(1)} %add_rsqrt_fusion.2) | copy-start | bytes 28
  20.0 12.4 %copy-start.44 = (f32[2048]{0:T(1024)S(1)}, f32[2048]{0:T(1024)}, u32[]{:S(2)}) copy-start(f32[2048]{0:T(1024)} %param.168) | copy-start | bytes 24580
  40.4 17.1 %copy-start.49 = (f32[3,2048]{1,0:T(4,128)S(1)}, f32[3,2048]{1,0:T(4,128)}, u32[]{:S(2)}) copy-start(f32[3,2048]{1,0:T(4,128)} %convert_reduce_fusion) | copy-start | bytes 73732
  60.7 59.8 %copy-start.16 = (f32[3,1152]{1,0:T(4,128)}, f32[3,1152]{1,0:T(4,128)S(1)}, u32[]{:S(2)}) copy-start(f32[3,1152]{1,0:T(4,128)S(1)} %get-tuple-element.392) | copy-start | bytes 41476
  60.7 59.8 %copy-start.55 = (f32[3]{0:T(128)}, f32[3]{0:T(128)S(1)}, u32[]{:S(2)}) copy-start(f32[3]{0:T(128)S(1)} %add_rsqrt_fusion.1) | copy-start | bytes 40
  62.7 6.6 collective-permute-start
  71.2 3.7 collective-permute-start
  76.8 5.0 collective-permute-start
  83.7 5.0 collective-permute-start
  90.6 5.0 collective-permute-start
  97.6 5.0 collective-permute-start
  104.5 5.0 collective-permute-start
  111.5 5.0 collective-permute-start
  131.7 14.9 %copy-start.6 = (bf16[3,7,13,2048]{3,2,1,0:T(8,128)(2,1)S(1)}, bf16[3,7,13,2048]{3,2,1,0:T(8,128)(2,1)}, u32[]{:S(2)}) copy-start(bf16[3,7,13,2048]{3,2,1,0:T(8,128)(2,1)} %get-tuple-element.334) | copy-start | bytes 3354628
  478.3 9.4 %copy-start.24 = (f32[7,2048]{1,0:T(8,128)S(1)}, f32[7,2048]{1,0:T(8,128)}, u32[]{:S(2)}) copy-start(f32[7,2048]{1,0:T(8,128)} %gather_fusion.7) | copy-start | bytes 172036
  478.4 9.5 %copy-start.20 = (f32[7,2048]{1,0:T(8,128)S(1)}, f32[7,2048]{1,0:T(8,128)}, u32[]{:S(2)}) copy-start(f32[7,2048]{1,0:T(8,128)} %gather_fusion.9) | copy-start | bytes 172036
  478.4 9.5 %copy-start.21 = (f32[7,2048]{1,0:T(8,128)S(1)}, f32[7,2048]{1,0:T(8,128)}, u32[]{:S(2)}) copy-start(f32[7,2048]{1,0:T(8,128)} %gather_fusion.10) | copy-start | bytes 172036
  478.4 9.6 %copy-start.22 = (f32[7,2048]{1,0:T(8,128)S(1)}, f32[7,2048]{1,0:T(8,128)}, u32[]{:S(2)}) copy-start(f32[7,2048]{1,0:T(8,128)} %gather_fusion.11) | copy-start | bytes 172036
  478.4 9.6 %copy-start.23 = (f32[7,2048]{1,0:T(8,128)S(1)}, f32[7,2048]{1,0:T(8,128)}, u32[]{:S(2)}) copy-start(f32[7,2048]{1,0:T(8,128)} %gather_fusion.12) | copy-start | bytes 172036
  478.4 9.6 %copy-start.25 = (f32[7,2048]{1,0:T(8,128)S(1)}, f32[7,2048]{1,0:T(8,128)}, u32[]{:S(2)}) copy-start(f32[7,2048]{1,0:T(8,128)} %gather_fusion.13) | copy-start | bytes 172036
  489.2 56.0 %copy-start.17 = (f32[3,1152]{1,0:T(4,128)S(1)}, f32[3,1152]{1,0:T(4,128)}, u32[]{:S(2)}) copy-start(f32[3,1152]{1,0:T(4,128)} %copy-done.16) | copy-start | bytes 41476
  489.2 56.0 %copy-start.46 = (f32[3,1152]{1,0:T(4,128)S(1)}, f32[3,1152]{1,0:T(4,128)}, u32[]{:S(2)}) copy-start(f32[3,1152]{1,0:T(4,128)} %copy-done.45) | copy-start | bytes 41476
  489.2 56.0 %copy-start.56 = (f32[3]{0:T(128)S(1)}, f32[3]{0:T(128)}, u32[]{:S(2)}) copy-start(f32[3]{0:T(128)} %copy-done.55) | copy-start | bytes 40
  489.2 56.0 %copy-start.61 = (f32[3]{0:T(128)S(1)}, f32[3]{0:T(128)}, u32[]{:S(2)}) copy-start(f32[3]{0:T(128)} %copy-done.60) | copy-start | bytes 40
  490.8 106.6 %all-reduce.9.cloned.1.call-start = ((), (), s32[]{:S(2)}) async-start(), calls=%async_computation.4 | async-start | bytes 917504 | tf_op jit(solution)/shard_map/psum | solution.py:15
  545.1 85.5 %reduce-scatter.8.cloned.1.call-start = ((), (), s32[]{:S(2)}) async-start(), calls=%async_computation.7 | async-start | bytes 2654208 | tf_op jit(solution)/shard_map/reduce_scatter | solution.py:199
  547.9 174.6 %reduce-scatter.4.cloned.1.call-start = ((), (), s32[]{:S(2)}) async-start(), calls=%async_computation.5 | async-start | bytes 9437184 | tf_op jit(solution)/shard_map/reduce_scatter | solution.py:197
  553.5 259.6 %reduce-scatter.6.cloned.1.call-start = ((), (), s32[]{:S(2)}) async-start(), calls=%async_computation.6 | async-start | bytes 9437184 | tf_op jit(solution)/shard_map/reduce_scatter | solution.py:198
  558.8 37.8 %copy-start.19 = (f32[4,1152]{1,0:T(4,128)S(1)}, f32[4,1152]{1,0:T(4,128)}, u32[]{:S(2)}) copy-start(f32[4,1152]{1,0:T(4,128)} %copy-done.18) | copy-start | bytes 55300
  558.8 37.8 %copy-start.52 = (bf16[2,1152]{1,0:T(2,128)(2,1)S(1)}, bf16[2,1152]{1,0:T(2,128)(2,1)}, u32[]{:S(2)}) copy-start(bf16[2,1152]{1,0:T(2,128)(2,1)} %param.164) | copy-start | bytes 13828
  558.8 37.8 %copy-start.59 = (f32[2]{0:T(128)S(1)}, f32[2]{0:T(128)}, u32[]{:S(2)}) copy-start(f32[2]{0:T(128)} %copy-done.58) | copy-start | bytes 28
  (45 other events, 220.6 us)
Sparse Core Ops, SparseCore 0:
  490.9 54.0 all-reduce.6
  548.4 45.2 all-reduce.8
  596.6 34.0 reduce-scatter.7
  633.4 89.0 reduce-scatter.3
  725.1 87.9 reduce-scatter.5
